TPU v7x, 128 devices: a whole 4x4x4 slice. The times are simulated.
128 devices in a mesh: grp: 8 (over y, core), dom: 16 (over z, x).
Axes of the slice: x: 4, y: 4, z: 4, core: 2. Of those that a mesh axis runs over, the one named last changes fastest.
Arguments:
- diag_blocks: bfloat16 [2048, 384, 384], P(('grp', 'dom')), may hold values from -0.3125 to 0.3125
- face_in: bfloat16 [4096, 384, 384], P(('grp', 'dom')), may hold values from -0.3125 to 0.3125
- face_cross: bfloat16 [2048, 384, 384], P(('grp', 'dom')), may hold values from -0.3125 to 0.3125
- metric: float32 [2048, 384], P(('grp', 'dom')), may hold values from 0.5 to 2
- source_in: int32 [4096], P(('grp', 'dom')), may hold values from 0 to 15
- source_cross: int32 [2048], P(('grp', 'dom')), may hold values from 0 to 15
- orient_in: int32 [4096], P(('grp', 'dom')), may hold values from 0 to 7
- orient_cross: int32 [2048], P(('grp', 'dom')), may hold values from 0 to 7
- peer_in: int32 [4096, 1], P(('grp', 'dom')), may hold values from 0 to 15; in each aligned block of 32 rows (0 to 31, 32 to 63, ...) at most 3 rows name the same one
- peer_cross: int32 [2048, 1], P(('grp', 'dom')), may hold values from 0 to 7; in each aligned block of 16 rows (0 to 15, 16 to 31, ...) at most 3 rows name the same one
- target_in: int32 [4096], P(('grp', 'dom')), may hold values from 0 to 47
- target_cross: int32 [2048], P(('grp', 'dom')), may hold values from 0 to 47
Outputs:
- coarse_diag: float32 [2048, 2304], P('grp')
- coarse_face: float32 [2048, 6912], P('grp')
Inputs may be any that keep to these rules, and one draw needn't show every extreme that they name: `peer_in`: at most 3 records of one device name the same partition; on some device exactly 3 do. `peer_cross`: at most 3 records of one device name the same group; on some device exactly 3 do.
All inputs are finite; a program needn't handle non-finite values.
Results may differ from a plain program's by a relative error of at most 0.0052.
Values may be sent and summed in bfloat16 or wider, within the bound.
A program may use at most 128 MiB of HBM per device.

v0:
```python
import jax
import jax.numpy as jnp
from jax import lax
from jax.sharding import PartitionSpec as P

CROSS_CAP = 3


def corner_table(var_count):
    nodes = -1.0 + 2.0 * jnp.arange(4, dtype=jnp.float32) / 3.0
    basis = jnp.stack(((1.0 - nodes) / 2.0, (1.0 + nodes) / 2.0), axis=1)
    cube = jnp.einsum("ia,jb,kc->abcijk", basis, basis, basis).reshape(8, 64)
    return jnp.kron(jnp.eye(var_count, dtype=jnp.float32), cube)


def restrictor(weights, orient):
    var_count = weights.shape[1] // 64
    table = corner_table(var_count)
    full = weights[:, None, :] * table[None]
    shaped = full.reshape(weights.shape[0], var_count * 8, var_count, 4, 4, 4)
    bits = orient.reshape(-1, 1, 1, 1, 1, 1)
    shaped = jnp.where(bits % 2 == 1, jnp.flip(shaped, 3), shaped)
    shaped = jnp.where(bits // 2 % 2 == 1, jnp.flip(shaped, 4), shaped)
    shaped = jnp.where(bits // 4 % 2 == 1, jnp.flip(shaped, 5), shaped)
    return shaped.reshape(weights.shape[0], var_count * 8, var_count * 64).astype(jnp.bfloat16)


def plain_restrictor(weights):
    table = corner_table(weights.shape[1] // 64)
    return (weights[:, None, :] * table[None]).astype(jnp.bfloat16)


def pick_rows(index, table):
    picks = (index[:, None] == jnp.arange(table.shape[0], dtype=jnp.int32)[None, :]).astype(
        jnp.float32
    )
    return jnp.dot(picks, table, precision=lax.Precision.HIGHEST)


def one_sided(blocks, column_side):
    return jnp.einsum(
        "rcj,rij->rci", column_side, blocks, preferred_element_type=jnp.float32
    ).astype(jnp.bfloat16)


def coarse_terms(row_side, products):
    return jnp.einsum("rci,rdi->rcd", row_side, products, preferred_element_type=jnp.float32)


def id_row(values, width):
    flat = values.reshape(-1).astype(jnp.bfloat16)
    return jnp.pad(flat, (0, width - flat.shape[0]))[None, :]


def per_device(
    diag_blocks,
    face_in,
    face_cross,
    metric,
    source_in,
    source_cross,
    orient_in,
    orient_cross,
    peer_in,
    peer_cross,
    target_in,
    target_cross,
):
    elem_count = metric.shape[0]
    coarse_width = metric.shape[1] // 8
    square = coarse_width * coarse_width
    slots_dev = 3 * elem_count
    group_width = lax.axis_size("dom")
    group_count = lax.axis_size("grp")
    my_dom = lax.axis_index("dom")
    my_grp = lax.axis_index("grp")
    inner_count = face_in.shape[0]
    cross_count = face_cross.shape[0]
    metric_dom = lax.all_gather(metric, "dom", axis=0, tiled=True)
    metric_grp = lax.all_gather(metric, "grp", axis=0, tiled=True)
    diag_side = plain_restrictor(metric)
    diag_c = coarse_terms(diag_side, one_sided(diag_blocks, diag_side))
    diag_rows = diag_c.reshape(elem_count, square).astype(jnp.bfloat16)
    diag_all = lax.all_gather(diag_rows, "dom", axis=0, tiled=True)
    cross_y = one_sided(face_cross, restrictor(pick_rows(source_cross, metric), orient_cross))
    peer_x = peer_cross[:, 0]
    cross_row_side = plain_restrictor(
        pick_rows(peer_x * elem_count + target_cross // 3, metric_grp)
    )
    cross_c = coarse_terms(cross_row_side, cross_y).reshape(cross_count, square)
    cross_ids = jnp.stack((peer_x, target_cross), axis=1)
    cross_packet = jnp.concatenate(
        (cross_c.astype(jnp.bfloat16), id_row(cross_ids, square)), axis=0
    )
    cross_got = lax.all_gather(cross_packet, "grp", axis=0)
    got_rows = cross_got[:, :cross_count, :]
    got_ids = cross_got[:, cross_count, : 2 * cross_count].astype(jnp.int32)
    got_peer = got_ids[:, 0::2]
    got_target = got_ids[:, 1::2]
    match = got_peer == my_grp
    rank = jnp.cumsum(match.astype(jnp.int32), axis=1) - 1
    picks = match[:, None, :] & (
        rank[:, None, :] == jnp.arange(CROSS_CAP, dtype=jnp.int32)[None, :, None]
    )
    mine_rows = (
        jnp.einsum(
            "skr,srq->skq", picks.astype(jnp.bfloat16), got_rows, preferred_element_type=jnp.float32
        )
        .astype(jnp.bfloat16)
        .reshape(group_count * CROSS_CAP, square)
    )
    mine_target = jnp.sum(jnp.where(picks, got_target[:, None, :], 0), axis=2)
    mine_slot = jnp.where(jnp.any(picks, axis=2), my_dom * slots_dev + mine_target, -1).reshape(-1)
    inner_y = one_sided(face_in, restrictor(pick_rows(source_in, metric), orient_in))
    peer_i = peer_in[:, 0]
    inner_row_side = plain_restrictor(pick_rows(peer_i * elem_count + target_in // 3, metric_dom))
    inner_c = coarse_terms(inner_row_side, inner_y).reshape(inner_count, square)
    inner_slot = peer_i * slots_dev + target_in
    slots = jnp.concatenate((inner_slot, mine_slot), axis=0)
    valid = slots >= 0
    slot_code = jnp.stack(
        (jnp.where(valid, slots // 32, -1), jnp.where(valid, slots % 32, 0)), axis=1
    )
    face_packet = jnp.concatenate(
        (inner_c.astype(jnp.bfloat16), mine_rows, id_row(slot_code, square)), axis=0
    )
    face_all = lax.all_gather(face_packet, "dom", axis=0)
    contrib_count = slots.shape[0]
    contrib = face_all[:, :contrib_count, :].reshape(group_width * contrib_count, square)
    codes = face_all[:, contrib_count, : 2 * contrib_count].astype(jnp.int32)
    hi = codes[:, 0::2].reshape(-1)
    lo = codes[:, 1::2].reshape(-1)
    got_slot = jnp.where(hi >= 0, hi * 32 + lo, -1)
    group_slots = group_width * slots_dev
    onehot = (jnp.arange(group_slots, dtype=jnp.int32)[:, None] == got_slot[None, :]).astype(
        jnp.bfloat16
    )
    face = jnp.dot(onehot, contrib, preferred_element_type=jnp.float32)
    coarse_diag = diag_all.astype(jnp.float32)
    coarse_face = face.reshape(group_width * elem_count, 3 * square)
    return (coarse_diag, coarse_face)


def solution(mesh):
    placed = (
        P(("grp", "dom"), None, None),
        P(("grp", "dom"), None, None),
        P(("grp", "dom"), None, None),
        P(("grp", "dom"), None),
        P(("grp", "dom")),
        P(("grp", "dom")),
        P(("grp", "dom")),
        P(("grp", "dom")),
        P(("grp", "dom"), None),
        P(("grp", "dom"), None),
        P(("grp", "dom")),
        P(("grp", "dom")),
    )
    return jax.shard_map(
        per_device,
        mesh=mesh,
        in_specs=placed,
        out_specs=(P("grp", None), P("grp", None)),
        check_vma=False,
    )
```

profile of v0, /device:TPU:1, one launch (start us, length us, event | category | flops | bytes accessed | tf_op | source)
XLA Modules:
  0.0 171.8 jit_solution(11630039760645675383)
XLA Ops:
  7.8 4.3 %fusion.26 = bf16[16,48,48]{2,1,0:T(8,128)(2,1)S(1)} fusion(bf16[16,384,384]{2,1,0:T(8,128)(2,1)} %param.12, f32[48,384]{1,0:T(8,128)S(1)} %mul.191, f32[16,384]{1,0:T(8,128)} %param.15), kind=kOutput, calls=%fused_computation.30 | convolution fusion | flops 256315392 | bytes 4890624 | tf_op jit(solution)/shard_map/rci,rdi->rcd/dot_general | solution.py:47
  12.0 0.9 convert_element_type.104
  13.2 14.6 %all_gather.23 = f32[128,384]{1,0:T(8,128)S(1)} all-gather(f32[16,384]{1,0:T(8,128)S(1)} %copy-done), channel_id=1, replica_groups=mesh['grp'=8,'dom'=16] {'grp'}, dimensions={0}, use_global_device_ids=true | all-gather | bytes 221184 | tf_op jit(solution)/shard_map/all_gather | solution.py:80
  28.1 0.4 fusion.43
  28.6 1.0 broadcast_multiply_fusion.1
  29.6 0.6 reverse_select_fusion.5
  30.2 0.7 reverse_select_fusion.4
  30.9 0.7 fusion.1
  31.6 0.2 fusion.42
  31.8 4.3 %fusion.27 = bf16[16,48,48]{2,1,0:T(8,128)(2,1)S(1)} fusion(bf16[16,384,384]{2,1,0:T(8,128)(2,1)} %param.14, bf16[16,48,384]{1,0,2:T(8,128)(2,1)S(1)} %bitcast.38, f32[16,384]{1,0:T(8,128)S(1)} %fusion.42, f32[48,384]{1,0:T(8,128)S(1)} %mul.191), kind=kOutput, calls=%fused_computation.31 | convolution fusion | flops 255725568 | bytes 5480448 | tf_op jit(solution)/shard_map/rci,rdi->rcd/dot_general | solution.py:47
  36.1 0.2 convert_element_type.117
  36.6 13.5 %all-gather.2 = bf16[8,17,2304]{2,1,0:T(8,128)(2,1)S(1)} all-gather(bf16[1,17,2304]{2,1,0:T(8,128)(2,1)S(1)} %maximum_bitcast_fusion.1), channel_id=2, replica_groups=mesh['grp'=8,'dom'=16] {'grp'}, dimensions={0}, use_global_device_ids=true | all-gather | bytes 705024 | tf_op jit(solution)/shard_map/all_gather | solution.py:95
  50.5 0.2 fusion.60
  50.7 0.2 convolution_convert_fusion
  50.9 20.3 %all_gather.22 = f32[256,384]{1,0:T(8,128)S(1)} all-gather(f32[16,384]{1,0:T(8,128)S(1)} %copy-done), channel_id=1, replica_groups=mesh['grp'=8,'dom'=16] {'dom'}, dimensions={0}, use_global_device_ids=true | all-gather | bytes 417792 | tf_op jit(solution)/shard_map/all_gather | solution.py:79
  71.2 0.2 select_reduce_fusion
  72.0 0.4 fusion.39
  72.4 1.9 %broadcast_multiply_fusion = bf16[32,48,6,4,4,4]{1,0,5,4,3,2:T(8,128)(2,1)S(1)} fusion(f32[48,6,4,4,4]{0,4,3,2,1:T(4,128)S(1)} %broadcast_multiply_fusion.2, f32[32,6,4,4,4]{0,4,3,2,1:T(4,128)S(1)} %bitcast.40), kind=kLoop, calls=%fused_computation.11 | loop fusion | flops 1179648 | bytes 1302528 | tf_op jit(solution)/shard_map/mul | solution.py:19
  74.4 0.3 fusion.37
  74.7 1.3 reverse_select_fusion.2
  76.0 1.5 reverse_select_fusion.1
  77.5 1.1 fusion
  78.6 8.9 %fusion.17 = bf16[32,48,48]{2,1,0:T(8,128)(2,1)} fusion(bf16[32,384,384]{2,1,0:T(8,128)(2,1)} %param.13, bf16[32,48,384]{1,0,2:T(8,128)(2,1)S(1)} %bitcast.37, f32[48,384]{1,0:T(8,128)S(1)} %mul.191, f32[32,384]{1,0:T(8,128)S(1)} %fusion.37), kind=kOutput, calls=%fused_computation.23 | convolution fusion | flops 511451136 | bytes 10887168 | tf_op jit(solution)/shard_map/rci,rdi->rcd/dot_general | solution.py:47
  87.5 1.4 convert_element_type.111
  88.9 0.7 maximum_bitcast_fusion
  89.7 2.8 %convert_element_type.105 = f32[256,2304]{1,0:T(8,128)} convert(bf16[256,2304]{1,0:T(8,128)(2,1)} %all-gather.7.cloned.1.call-done) | non-fusion elementwise | flops 589824 | bytes 3538944 | tf_op jit(solution)/shard_map/convert_element_type | solution.py:139
  92.5 54.4 %all-gather.9.cloned.1.call-done = bf16[16,57,2304]{2,1,0:T(8,128)(2,1)} async-done(((bf16[1,57,2304]{2,1,0:T(8,128)(2,1)}), bf16[16,57,2304]{2,1,0:T(8,128)(2,1)}) %all-gather.9.cloned.1.call-update) | async-done | bytes 4202512 | tf_op jit(solution)/shard_map/all_gather | solution.py:127
  146.9 0.8 slice_convert_fusion
  147.9 0.2 slice.30
  148.2 2.2 %slice-done = bf16[16,56,2304]{2,1,0:T(8,128)(2,1)S(1)} async-done(((bf16[16,57,2304]{2,1,0:T(8,128)(2,1)}), bf16[16,56,2304]{2,1,0:T(8,128)(2,1)S(1)}, s32[]{:S(2)}) %slice-start) | async-done | bytes 4128792 | tf_op jit(solution)/shard_map/slice | solution.py:129
  150.4 6.0 %fusion.4 = f32[768,2304]{1,0:T(8,128)} fusion(bf16[896,2304]{1,0:T(8,128)(2,1)S(1)} %bitcast.39, s32[896]{0:T(1024)S(1)} %select_n.198), kind=kOutput, calls=%fused_computation.13 | convolution fusion | flops 3171581952 | bytes 11210240 | tf_op jit(solution)/shard_map/dot_general | solution.py:138
  156.3 8.6 %reshape.527 = f32[256,6912]{1,0:T(8,128)} reshape(f32[768,2304]{1,0:T(8,128)} %fusion.4) | data formatting | bytes 14155776 | tf_op jit(solution)/shard_map/reshape | solution.py:140
  (68 shorter events, 2.6 us)
Async XLA Ops:
  7.2 6.0 %copy-start = (f32[16,384]{1,0:T(8,128)S(1)}, f32[16,384]{1,0:T(8,128)}, u32[]{:S(2)}) copy-start(f32[16,384]{1,0:T(8,128)} %param.15) | copy-start | bytes 73732
  7.2 82.5 %all-gather.7.cloned.1.call-start = ((), (), s32[]{:S(2)}) async-start(), calls=%async_computation | async-start | bytes 1253376 | tf_op jit(solution)/shard_map/all_gather | solution.py:84
  7.7 20.4 %copy-start.1 = (s32[16]{0:T(128)S(1)}, s32[16]{0:T(128)}, u32[]{:S(2)}) copy-start(s32[16]{0:T(128)} %param.17) | copy-start | bytes 196
  7.7 20.7 %copy-start.3 = (s32[16]{0:T(128)S(1)}, s32[16]{0:T(128)}, u32[]{:S(2)}) copy-start(s32[16]{0:T(128)} %param.19) | copy-start | bytes 196
  7.7 20.7 %copy-start.5 = (s32[16,1]{0,1:T(1,128)S(1)}, s32[16,1]{0,1:T(1,128)}, u32[]{:S(2)}) copy-start(s32[16,1]{0,1:T(1,128)} %param.21) | copy-start | bytes 196
  7.8 20.8 %copy-start.4 = (s32[16]{0:T(128)S(1)}, s32[16]{0:T(128)}, u32[]{:S(2)}) copy-start(s32[16]{0:T(128)} %param.23) | copy-start | bytes 196
  12.9 134.0 %all-gather.9.cloned.1.call-start = ((), (), s32[]{:S(2)}) async-start(), calls=%async_computation.1 | async-start | bytes 5013504 | tf_op jit(solution)/shard_map/all_gather | solution.py:127
  31.8 39.7 %copy-start.6 = (s32[32]{0:T(128)S(1)}, s32[32]{0:T(128)}, u32[]{:S(2)}) copy-start(s32[32]{0:T(128)} %param.22) | copy-start | bytes 388
  31.8 39.7 %copy-start.7 = (s32[32,1]{0,1:T(1,128)S(1)}, s32[32,1]{0,1:T(1,128)}, u32[]{:S(2)}) copy-start(s32[32,1]{0,1:T(1,128)} %param.20) | copy-start | bytes 388
  31.8 40.2 %copy-start.2 = (s32[32]{0:T(128)S(1)}, s32[32]{0:T(128)}, u32[]{:S(2)}) copy-start(s32[32]{0:T(128)} %param.16) | copy-start | bytes 388
  36.6 37.8 %copy-start.8 = (s32[32]{0:T(128)S(1)}, s32[32]{0:T(128)}, u32[]{:S(2)}) copy-start(s32[32]{0:T(128)} %param.18) | copy-start | bytes 388
  148.2 2.2 %slice-start = ((bf16[16,57,2304]{2,1,0:T(8,128)(2,1)}), bf16[16,56,2304]{2,1,0:T(8,128)(2,1)S(1)}, s32[]{:S(2)}) async-start(bf16[16,57,2304]{2,1,0:T(8,128)(2,1)} %all-gather.9.cloned.1.call-done), calls=%async_computation.2 | async-start | bytes 8257536 | tf_op jit(solution)/shard_map/slice | solution.py:129
Sparse Core Ops, SparseCore 0:
  13.0 44.4 all-gather.6
  89.8 57.1 all-gather.8
where the time goes:
time: 172 us
  waiting for transfers between devices  54.5 us (32%)
  blocking collectives  48.4 us (28%)
  matrix products  24.8 us (14%)
  local copies, waits for them, and re-layouts  15.2 us (9%)
  between operations  14.4 us (8%)
  other arithmetic  14.3 us (8%)
    all_gather x1, waiting for transfers between devices, per_device(): face_all = lax.all_gather(face_packet, 'dom', axis=0)  54.4 us
    all_gather x1, blocking collectives, per_device(): metric_dom = lax.all_gather(metric, 'dom', axis=0, tiled=True)  20.3 us
    dot_general x3, matrix products, coarse_terms(): jnp.einsum('rci,rdi->rcd', row_side, products, preferred_element_type=jnp...  17.4 us
    all_gather x1, blocking collectives, per_device(): metric_grp = lax.all_gather(metric, 'grp', axis=0, tiled=True)  14.6 us
    all_gather x1, blocking collectives, per_device(): cross_got = lax.all_gather(cross_packet, 'grp', axis=0)  13.5 us
    reshape x1, local copies, waits for them, and re-layouts, per_device(): coarse_face = face.reshape(group_width * elem_count, 3 * square)  8.64 us
    dot_general x1, matrix products, per_device(): face = jnp.dot(onehot, contrib, preferred_element_type=jnp.float32)  5.97 us
  transfers between devices with their start and end apart: 2, of which 1 were waited for; matrix products, arithmetic and copies ran while one was open for 18% of the time, Pallas kernels for 0%

commit v1 on v0

--- a/solution.py
+++ b/solution.py
@@ -4,6 +4,22 @@
 from jax.sharding import PartitionSpec as P
 
 CROSS_CAP = 3
+
+
+def collect(x, axis, dim):
+    ways, here, step = (lax.axis_size(axis), lax.axis_index(axis), x.shape[dim])
+    dims = [n * ways if d == dim else n for d, n in enumerate(x.shape)]
+    full = lax.dynamic_update_slice_in_dim(jnp.zeros(dims, x.dtype), x, here * step, axis=dim)
+    going_up = going_down = x
+    for far in range(1, ways // 2 + 1):
+        going_up = lax.ppermute(going_up, axis, [(d, (d + 1) % ways) for d in range(ways)])
+        full = lax.dynamic_update_slice_in_dim(full, going_up, (here - far) % ways * step, axis=dim)
+        if 2 * far < ways:
+            going_down = lax.ppermute(going_down, axis, [(d, (d - 1) % ways) for d in range(ways)])
+            full = lax.dynamic_update_slice_in_dim(
+                full, going_down, (here + far) % ways * step, axis=dim
+            )
+    return full
 
 
 def corner_table(var_count):
@@ -76,7 +92,7 @@
     my_grp = lax.axis_index("grp")
     inner_count = face_in.shape[0]
     cross_count = face_cross.shape[0]
-    metric_dom = lax.all_gather(metric, "dom", axis=0, tiled=True)
+    metric_dom = collect(metric, "dom", 0)
     metric_grp = lax.all_gather(metric, "grp", axis=0, tiled=True)
     diag_side = plain_restrictor(metric)
     diag_c = coarse_terms(diag_side, one_sided(diag_blocks, diag_side))

time: 172 us -> 205 us (1.19)
  starting transfers between devices: 0.08 us -> 35.8 us
  blocking collectives: 48.4 us -> 28.8 us
  local copies, waits for them, and re-layouts: 15.2 us -> 25.1 us
  waiting for transfers between devices: 54.5 us -> 59.1 us
    ppermute x0 -> x15, starting transfers between devices: none -> 35.7 us  [the longest x7 33.5 us: collect(): lax.ppermute(going_down, axis, [(d, (d - 1) % ways) for d in range(ways)])]
    all_gather x1 -> x0, blocking collectives: 20.3 us -> none  [per_device(): metric_dom = lax.all_gather(metric, 'dom', axis=0, tiled=True)]
    dynamic_update_slice x0 -> x16, local copies, waits for them, and re-layouts: none -> 9.15 us  [the longest x8 4.87 us: collect(): lax.dynamic_update_slice_in_dim(full, going_up, (here - far) % ways * ste...]
    ppermute x0 -> x15, waiting for transfers between devices: none -> 4.81 us  [the longest x8 4.79 us: collect(): lax.ppermute(going_up, axis, [(d, (d + 1) % ways) for d in range(ways)])]
  transfers between devices with their start and end apart: 2 -> 17, of which waited for: 1 -> 2; matrix products, arithmetic and copies ran while one was open for 18% -> 23% of each run, Pallas kernels for 0% -> 0%
where the time goes in v1:
time: 205 us
  waiting for transfers between devices  59.1 us (29%)
  starting transfers between devices  35.8 us (17%)
  blocking collectives  28.8 us (14%)
  matrix products  26.5 us (13%)
  local copies, waits for them, and re-layouts  25.1 us (12%)
  between operations  14.9 us (7%)
  other arithmetic  14.6 us (7%)
    all_gather x1, waiting for transfers between devices, per_device(): face_all = lax.all_gather(face_packet, 'dom', axis=0)  54.3 us
    ppermute x7, starting transfers between devices, collect(): lax.ppermute(going_down, axis, [(d, (d - 1) % ways) for d in range(ways)])  33.5 us
    dot_general x3, matrix products, coarse_terms(): jnp.einsum('rci,rdi->rcd', row_side, products, preferred_element_type=jnp...  17.4 us
    all_gather x1, blocking collectives, per_device(): metric_grp = lax.all_gather(metric, 'grp', axis=0, tiled=True)  15.2 us
    all_gather x1, blocking collectives, per_device(): cross_got = lax.all_gather(cross_packet, 'grp', axis=0)  13.7 us
    reshape x1, local copies, waits for them, and re-layouts, per_device(): coarse_face = face.reshape(group_width * elem_count, 3 * square)  8.64 us
    dot_general x1, matrix products, per_device(): face = jnp.dot(onehot, contrib, preferred_element_type=jnp.float32)  5.98 us
    dynamic_update_slice x8, local copies, waits for them, and re-layouts, collect(): lax.dynamic_update_slice_in_dim(full, going_up, (here - far) % ways * ste...  4.87 us
  transfers between devices with their start and end apart: 17, of which 2 were waited for; matrix products, arithmetic and copies ran while one was open for 23% of the time, Pallas kernels for 0%

profile of v1, /device:TPU:1, one launch (start us, length us, event | category | flops | bytes accessed | tf_op | source)
XLA Modules:
  0.0 204.9 jit_solution(15847165574928504634)
XLA Ops:
  7.2 2.1 %collective-permute-start = (f32[16,384]{1,0:T(8,128)}, f32[16,384]{1,0:T(8,128)S(1)}, u32[]{:S(2)}, u32[]{:S(2)}) collective-permute-start(f32[16,384]{1,0:T(8,128)} %param.15), channel_id=1, source_target_pairs={{0,1},{1,2},{2,3},{3,4},{4,5},{5,6},{6,7},{7,8},{8,9},{9,10},{10,1... | collective-permute-start | bytes 73736 | tf_op jit(solution)/shard_map/ppermute | solution.py:15
  9.3 4.8 %collective-permute-start.1 = (f32[16,384]{1,0:T(8,128)}, f32[16,384]{1,0:T(8,128)S(1)}, u32[]{:S(2)}, u32[]{:S(2)}) collective-permute-start(f32[16,384]{1,0:T(8,128)} %param.15), channel_id=1, source_target_pairs={{0,15},{1,0},{2,1},{3,2},{4,3},{5,4},{6,5},{7,6},{8,7},{9,8},{10,9... | collective-permute-start | bytes 73736 | tf_op jit(solution)/shard_map/ppermute | solution.py:18
  14.7 4.3 %fusion.26 = bf16[16,48,48]{2,1,0:T(8,128)(2,1)S(1)} fusion(bf16[16,384,384]{2,1,0:T(8,128)(2,1)} %param.12, f32[48,384]{1,0:T(8,128)S(1)} %mul.239, f32[16,384]{1,0:T(8,128)} %param.15), kind=kOutput, calls=%fused_computation.30 | convolution fusion | flops 256315392 | bytes 4890624 | tf_op jit(solution)/shard_map/rci,rdi->rcd/dot_general | solution.py:63
  19.0 0.9 convert_element_type.104
  20.1 15.2 %all_gather.19 = f32[128,384]{1,0:T(8,128)} all-gather(f32[16,384]{1,0:T(8,128)S(1)} %copy-done.1), channel_id=1, replica_groups=mesh['grp'=8,'dom'=16] {'grp'}, dimensions={0}, use_global_device_ids=true | all-gather | bytes 221184 | tf_op jit(solution)/shard_map/all_gather | solution.py:96
  36.0 1.0 broadcast_multiply_fusion.1
  37.6 0.7 reverse_select_fusion.4
  39.2 4.3 %fusion.27 = bf16[16,48,48]{2,1,0:T(8,128)(2,1)S(1)} fusion(bf16[16,384,384]{2,1,0:T(8,128)(2,1)} %param.14, bf16[16,48,384]{1,0,2:T(8,128)(2,1)S(1)} %bitcast.38, f32[16,384]{1,0:T(8,128)S(1)} %fusion.42, f32[48,384]{1,0:T(8,128)S(1)} %mul.239), kind=kOutput, calls=%fused_computation.31 | convolution fusion | flops 255725568 | bytes 5480448 | tf_op jit(solution)/shard_map/rci,rdi->rcd/dot_general | solution.py:63
  44.0 13.7 %all-gather.2 = bf16[8,17,2304]{2,1,0:T(8,128)(2,1)S(1)} all-gather(bf16[1,17,2304]{2,1,0:T(8,128)(2,1)S(1)} %maximum_bitcast_fusion.1), channel_id=2, replica_groups=mesh['grp'=8,'dom'=16] {'grp'}, dimensions={0}, use_global_device_ids=true | all-gather | bytes 705024 | tf_op jit(solution)/shard_map/all_gather | solution.py:111
  58.3 0.9 convolution_convert_fusion
  59.5 1.9 broadcast_multiply_fusion
  61.9 0.7 copy-done
  62.7 1.3 reverse_select_fusion.2
  64.0 1.5 reverse_select_fusion.1
  65.5 1.5 fusion
  67.9 4.8 %collective-permute-start.3 = (f32[16,384]{1,0:T(8,128)S(1)}, f32[16,384]{1,0:T(8,128)S(1)}, u32[]{:S(2)}, u32[]{:S(2)}) collective-permute-start(f32[16,384]{1,0:T(8,128)S(1)} %collective-permute-done.1), channel_id=1, source_target_pairs={{0,15},{1,0},{2,1},{3,2},{4,3},{5,4},{6,5},{7,6},{8,7},{9,8},{10,9... | collective-permute-start | bytes 73736 | tf_op jit(solution)/shard_map/ppermute | solution.py:18
  73.9 4.8 %collective-permute-start.5 = (f32[16,384]{1,0:T(8,128)S(1)}, f32[16,384]{1,0:T(8,128)S(1)}, u32[]{:S(2)}, u32[]{:S(2)}) collective-permute-start(f32[16,384]{1,0:T(8,128)S(1)} %collective-permute-done.3), channel_id=1, source_target_pairs={{0,15},{1,0},{2,1},{3,2},{4,3},{5,4},{6,5},{7,6},{8,7},{9,8},{10,9... | collective-permute-start | bytes 73736 | tf_op jit(solution)/shard_map/ppermute | solution.py:18
  79.9 4.8 %collective-permute-start.7 = (f32[16,384]{1,0:T(8,128)S(1)}, f32[16,384]{1,0:T(8,128)S(1)}, u32[]{:S(2)}, u32[]{:S(2)}) collective-permute-start(f32[16,384]{1,0:T(8,128)S(1)} %collective-permute-done.5), channel_id=1, source_target_pairs={{0,15},{1,0},{2,1},{3,2},{4,3},{5,4},{6,5},{7,6},{8,7},{9,8},{10,9... | collective-permute-start | bytes 73736 | tf_op jit(solution)/shard_map/ppermute | solution.py:18
  85.9 4.8 %collective-permute-start.9 = (f32[16,384]{1,0:T(8,128)S(1)}, f32[16,384]{1,0:T(8,128)S(1)}, u32[]{:S(2)}, u32[]{:S(2)}) collective-permute-start(f32[16,384]{1,0:T(8,128)S(1)} %collective-permute-done.7), channel_id=1, source_target_pairs={{0,15},{1,0},{2,1},{3,2},{4,3},{5,4},{6,5},{7,6},{8,7},{9,8},{10,9... | collective-permute-start | bytes 73736 | tf_op jit(solution)/shard_map/ppermute | solution.py:18
  92.0 4.8 %collective-permute-start.11 = (f32[16,384]{1,0:T(8,128)S(1)}, f32[16,384]{1,0:T(8,128)S(1)}, u32[]{:S(2)}, u32[]{:S(2)}) collective-permute-start(f32[16,384]{1,0:T(8,128)S(1)} %collective-permute-done.9), channel_id=1, source_target_pairs={{0,15},{1,0},{2,1},{3,2},{4,3},{5,4},{6,5},{7,6},{8,7},{9,8},{10,9... | collective-permute-start | bytes 73736 | tf_op jit(solution)/shard_map/ppermute | solution.py:18
  98.0 4.8 %collective-permute-start.13 = (f32[16,384]{1,0:T(8,128)S(1)}, f32[16,384]{1,0:T(8,128)S(1)}, u32[]{:S(2)}, u32[]{:S(2)}) collective-permute-start(f32[16,384]{1,0:T(8,128)S(1)} %collective-permute-done.11), channel_id=1, source_target_pairs={{0,15},{1,0},{2,1},{3,2},{4,3},{5,4},{6,5},{7,6},{8,7},{9,8},{10,9... | collective-permute-start | bytes 73736 | tf_op jit(solution)/shard_map/ppermute | solution.py:18
  105.2 4.8 %collective-permute-done.14 = f32[16,384]{1,0:T(8,128)S(1)} collective-permute-done((f32[16,384]{1,0:T(8,128)S(1)}, f32[16,384]{1,0:T(8,128)S(1)}, u32[]{:S(2)}, u32[]{:S(2)}) %collective-permute-start.14) | collective-permute-done | bytes 24608 | tf_op jit(solution)/shard_map/ppermute | solution.py:15
  110.6 1.3 fusion.37
  111.8 8.9 %fusion.17 = bf16[32,48,48]{2,1,0:T(8,128)(2,1)} fusion(bf16[32,384,384]{2,1,0:T(8,128)(2,1)} %param.13, bf16[32,48,384]{1,0,2:T(8,128)(2,1)S(1)} %bitcast.37, f32[48,384]{1,0:T(8,128)S(1)} %mul.239, f32[32,384]{1,0:T(8,128)S(1)} %fusion.37), kind=kOutput, calls=%fused_computation.23 | convolution fusion | flops 511451136 | bytes 10887168 | tf_op jit(solution)/shard_map/rci,rdi->rcd/dot_general | solution.py:63
  120.7 1.4 convert_element_type.111
  122.1 0.7 maximum_bitcast_fusion
  122.9 2.8 %convert_element_type.105 = f32[256,2304]{1,0:T(8,128)} convert(bf16[256,2304]{1,0:T(8,128)(2,1)} %all-gather.7.cloned.1.call-done) | non-fusion elementwise | flops 589824 | bytes 3538944 | tf_op jit(solution)/shard_map/convert_element_type | solution.py:155
  125.7 54.3 %all-gather.9.cloned.1.call-done = bf16[16,57,2304]{2,1,0:T(8,128)(2,1)} async-done(((bf16[1,57,2304]{2,1,0:T(8,128)(2,1)}), bf16[16,57,2304]{2,1,0:T(8,128)(2,1)}) %all-gather.9.cloned.1.call-update) | async-done | bytes 4202512 | tf_op jit(solution)/shard_map/all_gather | solution.py:143
  180.0 0.8 slice_convert_fusion
  181.2 2.2 %slice-done = bf16[16,56,2304]{2,1,0:T(8,128)(2,1)S(1)} async-done(((bf16[16,57,2304]{2,1,0:T(8,128)(2,1)}), bf16[16,56,2304]{2,1,0:T(8,128)(2,1)S(1)}, s32[]{:S(2)}) %slice-start) | async-done | bytes 4128792 | tf_op jit(solution)/shard_map/slice | solution.py:145
  183.4 6.0 %fusion.4 = f32[768,2304]{1,0:T(8,128)} fusion(bf16[896,2304]{1,0:T(8,128)(2,1)S(1)} %bitcast.39, s32[896]{0:T(1024)S(1)} %select_n.339), kind=kOutput, calls=%fused_computation.13 | convolution fusion | flops 3171581952 | bytes 11210240 | tf_op jit(solution)/shard_map/dot_general | solution.py:154
  189.4 8.6 %reshape.527 = f32[256,6912]{1,0:T(8,128)} reshape(f32[768,2304]{1,0:T(8,128)} %fusion.4) | data formatting | bytes 14155776 | tf_op jit(solution)/shard_map/reshape | solution.py:156
  (120 shorter events, 14.9 us)
Async XLA Ops:
  7.2 12.9 %copy-start.1 = (f32[16,384]{1,0:T(8,128)S(1)}, f32[16,384]{1,0:T(8,128)}, u32[]{:S(2)}) copy-start(f32[16,384]{1,0:T(8,128)} %param.15) | copy-start | bytes 73732
  7.2 115.7 %all-gather.7.cloned.1.call-start = ((), (), s32[]{:S(2)}) async-start(), calls=%async_computation | async-start | bytes 1253376 | tf_op jit(solution)/shard_map/all_gather | solution.py:100
  7.2 60.6 %collective-permute-start = (f32[16,384]{1,0:T(8,128)}, f32[16,384]{1,0:T(8,128)S(1)}, u32[]{:S(2)}, u32[]{:S(2)}) collective-permute-start(f32[16,384]{1,0:T(8,128)} %param.15), channel_id=1, source_target_pairs={{0,1},{1,2},{2,3},{3,4},{4,5},{5,6},{6,7},{7,8},{8,9},{9,10},{10,1... | collective-permute-start | bytes 73736 | tf_op jit(solution)/shard_map/ppermute | solution.py:15
  9.3 58.6 %collective-permute-start.1 = (f32[16,384]{1,0:T(8,128)}, f32[16,384]{1,0:T(8,128)S(1)}, u32[]{:S(2)}, u32[]{:S(2)}) collective-permute-start(f32[16,384]{1,0:T(8,128)} %param.15), channel_id=1, source_target_pairs={{0,15},{1,0},{2,1},{3,2},{4,3},{5,4},{6,5},{7,6},{8,7},{9,8},{10,9... | collective-permute-start | bytes 73736 | tf_op jit(solution)/shard_map/ppermute | solution.py:18
  14.6 20.9 %copy-start.4 = (s32[16]{0:T(128)S(1)}, s32[16]{0:T(128)}, u32[]{:S(2)}) copy-start(s32[16]{0:T(128)} %param.17) | copy-start | bytes 196
  14.6 21.3 %copy-start.6 = (s32[16]{0:T(128)S(1)}, s32[16]{0:T(128)}, u32[]{:S(2)}) copy-start(s32[16]{0:T(128)} %param.19) | copy-start | bytes 196
  14.6 21.3 %copy-start.8 = (s32[16,1]{0,1:T(1,128)S(1)}, s32[16,1]{0,1:T(1,128)}, u32[]{:S(2)}) copy-start(s32[16,1]{0,1:T(1,128)} %param.21) | copy-start | bytes 196
  14.7 21.3 %copy-start.7 = (s32[16]{0:T(128)S(1)}, s32[16]{0:T(128)}, u32[]{:S(2)}) copy-start(s32[16]{0:T(128)} %param.23) | copy-start | bytes 196
  19.8 160.1 %all-gather.9.cloned.1.call-start = ((), (), s32[]{:S(2)}) async-start(), calls=%async_computation.1 | async-start | bytes 5013504 | tf_op jit(solution)/shard_map/all_gather | solution.py:143
  37.6 1.3 copy-start.2
  39.2 20.0 %copy-start.5 = (s32[32]{0:T(128)S(1)}, s32[32]{0:T(128)}, u32[]{:S(2)}) copy-start(s32[32]{0:T(128)} %param.16) | copy-start | bytes 388
  43.5 18.0 %copy-start.9 = (s32[32]{0:T(128)S(1)}, s32[32]{0:T(128)}, u32[]{:S(2)}) copy-start(s32[32]{0:T(128)} %param.18) | copy-start | bytes 388
  43.7 18.2 %copy-start.10 = (s32[32]{0:T(128)S(1)}, s32[32]{0:T(128)}, u32[]{:S(2)}) copy-start(s32[32]{0:T(128)} %param.22) | copy-start | bytes 388
  43.7 18.2 %copy-start.11 = (s32[32,1]{0,1:T(1,128)S(1)}, s32[32,1]{0,1:T(1,128)}, u32[]{:S(2)}) copy-start(s32[32,1]{0,1:T(1,128)} %param.20) | copy-start | bytes 388
  61.9 0.7 copy-start
  65.5 2.2 %copy-start.3 = (bf16[8,3,2304]{2,1,0:T(4,128)(2,1)S(1)}, bf16[8,3,2304]{2,1,0:T(4,128)(2,1)}, u32[]{:S(2)}) copy-start(bf16[8,3,2304]{2,1,0:T(4,128)(2,1)} %convolution_convert_fusion) | copy-start | bytes 331780
  67.8 6.1 %collective-permute-start.2 = (f32[16,384]{1,0:T(8,128)S(1)}, f32[16,384]{1,0:T(8,128)S(1)}, u32[]{:S(2)}, u32[]{:S(2)}) collective-permute-start(f32[16,384]{1,0:T(8,128)S(1)} %collective-permute-done), channel_id=1, source_target_pairs={{0,1},{1,2},{2,3},{3,4},{4,5},{5,6},{6,7},{7,8},{8,9},{9,10},{10,1... | collective-permute-start | bytes 73736 | tf_op jit(solution)/shard_map/ppermute | solution.py:15
  67.9 6.0 %collective-permute-start.3 = (f32[16,384]{1,0:T(8,128)S(1)}, f32[16,384]{1,0:T(8,128)S(1)}, u32[]{:S(2)}, u32[]{:S(2)}) collective-permute-start(f32[16,384]{1,0:T(8,128)S(1)} %collective-permute-done.1), channel_id=1, source_target_pairs={{0,15},{1,0},{2,1},{3,2},{4,3},{5,4},{6,5},{7,6},{8,7},{9,8},{10,9... | collective-permute-start | bytes 73736 | tf_op jit(solution)/shard_map/ppermute | solution.py:18
  73.9 6.0 %collective-permute-start.4 = (f32[16,384]{1,0:T(8,128)S(1)}, f32[16,384]{1,0:T(8,128)S(1)}, u32[]{:S(2)}, u32[]{:S(2)}) collective-permute-start(f32[16,384]{1,0:T(8,128)S(1)} %collective-permute-done.2), channel_id=1, source_target_pairs={{0,1},{1,2},{2,3},{3,4},{4,5},{5,6},{6,7},{7,8},{8,9},{9,10},{10,1... | collective-permute-start | bytes 73736 | tf_op jit(solution)/shard_map/ppermute | solution.py:15
  73.9 6.0 %collective-permute-start.5 = (f32[16,384]{1,0:T(8,128)S(1)}, f32[16,384]{1,0:T(8,128)S(1)}, u32[]{:S(2)}, u32[]{:S(2)}) collective-permute-start(f32[16,384]{1,0:T(8,128)S(1)} %collective-permute-done.3), channel_id=1, source_target_pairs={{0,15},{1,0},{2,1},{3,2},{4,3},{5,4},{6,5},{7,6},{8,7},{9,8},{10,9... | collective-permute-start | bytes 73736 | tf_op jit(solution)/shard_map/ppermute | solution.py:18
  79.9 6.0 %collective-permute-start.6 = (f32[16,384]{1,0:T(8,128)S(1)}, f32[16,384]{1,0:T(8,128)S(1)}, u32[]{:S(2)}, u32[]{:S(2)}) collective-permute-start(f32[16,384]{1,0:T(8,128)S(1)} %collective-permute-done.4), channel_id=1, source_target_pairs={{0,1},{1,2},{2,3},{3,4},{4,5},{5,6},{6,7},{7,8},{8,9},{9,10},{10,1... | collective-permute-start | bytes 73736 | tf_op jit(solution)/shard_map/ppermute | solution.py:15
  79.9 6.0 %collective-permute-start.7 = (f32[16,384]{1,0:T(8,128)S(1)}, f32[16,384]{1,0:T(8,128)S(1)}, u32[]{:S(2)}, u32[]{:S(2)}) collective-permute-start(f32[16,384]{1,0:T(8,128)S(1)} %collective-permute-done.5), channel_id=1, source_target_pairs={{0,15},{1,0},{2,1},{3,2},{4,3},{5,4},{6,5},{7,6},{8,7},{9,8},{10,9... | collective-permute-start | bytes 73736 | tf_op jit(solution)/shard_map/ppermute | solution.py:18
  85.9 6.0 %collective-permute-start.8 = (f32[16,384]{1,0:T(8,128)S(1)}, f32[16,384]{1,0:T(8,128)S(1)}, u32[]{:S(2)}, u32[]{:S(2)}) collective-permute-start(f32[16,384]{1,0:T(8,128)S(1)} %collective-permute-done.6), channel_id=1, source_target_pairs={{0,1},{1,2},{2,3},{3,4},{4,5},{5,6},{6,7},{7,8},{8,9},{9,10},{10,1... | collective-permute-start | bytes 73736 | tf_op jit(solution)/shard_map/ppermute | solution.py:15
  85.9 6.0 %collective-permute-start.9 = (f32[16,384]{1,0:T(8,128)S(1)}, f32[16,384]{1,0:T(8,128)S(1)}, u32[]{:S(2)}, u32[]{:S(2)}) collective-permute-start(f32[16,384]{1,0:T(8,128)S(1)} %collective-permute-done.7), channel_id=1, source_target_pairs={{0,15},{1,0},{2,1},{3,2},{4,3},{5,4},{6,5},{7,6},{8,7},{9,8},{10,9... | collective-permute-start | bytes 73736 | tf_op jit(solution)/shard_map/ppermute | solution.py:18
  91.9 6.0 %collective-permute-start.10 = (f32[16,384]{1,0:T(8,128)S(1)}, f32[16,384]{1,0:T(8,128)S(1)}, u32[]{:S(2)}, u32[]{:S(2)}) collective-permute-start(f32[16,384]{1,0:T(8,128)S(1)} %collective-permute-done.8), channel_id=1, source_target_pairs={{0,1},{1,2},{2,3},{3,4},{4,5},{5,6},{6,7},{7,8},{8,9},{9,10},{10,1... | collective-permute-start | bytes 73736 | tf_op jit(solution)/shard_map/ppermute | solution.py:15
  92.0 6.0 %collective-permute-start.11 = (f32[16,384]{1,0:T(8,128)S(1)}, f32[16,384]{1,0:T(8,128)S(1)}, u32[]{:S(2)}, u32[]{:S(2)}) collective-permute-start(f32[16,384]{1,0:T(8,128)S(1)} %collective-permute-done.9), channel_id=1, source_target_pairs={{0,15},{1,0},{2,1},{3,2},{4,3},{5,4},{6,5},{7,6},{8,7},{9,8},{10,9... | collective-permute-start | bytes 73736 | tf_op jit(solution)/shard_map/ppermute | solution.py:18
  98.0 6.0 %collective-permute-start.12 = (f32[16,384]{1,0:T(8,128)S(1)}, f32[16,384]{1,0:T(8,128)S(1)}, u32[]{:S(2)}, u32[]{:S(2)}) collective-permute-start(f32[16,384]{1,0:T(8,128)S(1)} %collective-permute-done.10), channel_id=1, source_target_pairs={{0,1},{1,2},{2,3},{3,4},{4,5},{5,6},{6,7},{7,8},{8,9},{9,10},{10,1... | collective-permute-start | bytes 73736 | tf_op jit(solution)/shard_map/ppermute | solution.py:15
  98.0 6.6 %collective-permute-start.13 = (f32[16,384]{1,0:T(8,128)S(1)}, f32[16,384]{1,0:T(8,128)S(1)}, u32[]{:S(2)}, u32[]{:S(2)}) collective-permute-start(f32[16,384]{1,0:T(8,128)S(1)} %collective-permute-done.11), channel_id=1, source_target_pairs={{0,15},{1,0},{2,1},{3,2},{4,3},{5,4},{6,5},{7,6},{8,7},{9,8},{10,9... | collective-permute-start | bytes 73736 | tf_op jit(solution)/shard_map/ppermute | solution.py:18
  104.0 6.0 %collective-permute-start.14 = (f32[16,384]{1,0:T(8,128)S(1)}, f32[16,384]{1,0:T(8,128)S(1)}, u32[]{:S(2)}, u32[]{:S(2)}) collective-permute-start(f32[16,384]{1,0:T(8,128)S(1)} %collective-permute-done.12), channel_id=1, source_target_pairs={{0,1},{1,2},{2,3},{3,4},{4,5},{5,6},{6,7},{7,8},{8,9},{9,10},{10,1... | collective-permute-start | bytes 73736 | tf_op jit(solution)/shard_map/ppermute | solution.py:15
  181.2 2.2 %slice-start = ((bf16[16,57,2304]{2,1,0:T(8,128)(2,1)}), bf16[16,56,2304]{2,1,0:T(8,128)(2,1)S(1)}, s32[]{:S(2)}) async-start(bf16[16,57,2304]{2,1,0:T(8,128)(2,1)} %all-gather.9.cloned.1.call-done), calls=%async_computation.2 | async-start | bytes 8257536 | tf_op jit(solution)/shard_map/slice | solution.py:145
Sparse Core Ops, SparseCore 0:
  20.0 39.7 all-gather.6
  123.0 56.9 all-gather.8
